TPU v7x, 32 devices: a whole 2x2x4 slice. The times are simulated.
32 devices in a mesh: probe: 4 (over y, core), store: 8 (over z, x).
Axes of the slice: x: 2, y: 2, z: 4, core: 2. Of those that a mesh axis runs over, the one named last changes fastest.
Arguments:
- probe_field: bfloat16 [96, 128, 8, 128], P('probe', 'store'), may hold values from -6 to 6
- bounds: int32 [96, 2], P('probe'), may hold values from 0 to 128, as said below
- courant: float32 [128, 8, 128], P('store'), may hold values from 0.1 to 0.2
- snapshots: bfloat16 [8, 128, 8, 128], P(None, 'store', 'probe'), may hold values from -0.5 to 0.5
- snap_times: int32 [8], replicated, may hold values from 0 to 7, each once
- basis_panels: bfloat16 [96, 128, 8, 128], P('probe', 'store'), may hold values from -0.015625 to 0.015625
Outputs:
- response: float32 [96, 128, 8, 128], P('probe', 'store')
- projection: float32 [96, 96], P(None, 'probe')
Inputs may be any that keep to these rules, and one draw needn't show every extreme that they name: 0 <= bounds[k, 0] < bounds[k, 1] <= 128 for every probe k, and each region holds at least 32 rows.
All inputs are finite; a program needn't handle non-finite values.
Results may differ from a plain program's by a relative error of at most 0.0031.
Values may be sent and summed in bfloat16 or wider, within the bound.
No kernel may reach another device: no remote copies, remote signals or barrier semaphores. Data moves between devices by JAX's collectives and lax.ppermute only.
A program may use at most 64 MiB of HBM per device.

v0:
```python
import jax
import jax.numpy as jnp
from jax import lax
from jax.sharding import PartitionSpec as P

stencil_taps = (-205.0 / 72.0, 8.0 / 5.0, -1.0 / 5.0, 8.0 / 315.0, -1.0 / 560.0)


def extended(x, sides, width):
    for axis, dim in sides:
        devices, length = (lax.axis_size(axis), x.shape[dim])
        up = [(i, (i + 1) % devices) for i in range(devices - 1)]
        down = [(j, i) for i, j in up]
        last = lax.slice_in_dim(x, length - width, length, axis=dim)
        leading = lax.slice_in_dim(x, 0, width, axis=dim)
        before = lax.ppermute(last, axis, up)
        after = lax.ppermute(leading, axis, down)
        x = jnp.concatenate([before, x, after], axis=dim)
    return x


def laplace(full):
    extent_x = full.shape[-3] - 8
    extent_y = full.shape[-2] - 8
    extent_z = full.shape[-1] - 8
    centre = full[..., 4 : 4 + extent_x, 4 : 4 + extent_y, 4 : 4 + extent_z]
    totals = 3.0 * stencil_taps[0] * centre
    for distance in range(1, 5):
        along = full[
            ..., 4 + distance : 4 + distance + extent_x, 4 : 4 + extent_y, 4 : 4 + extent_z
        ]
        along = (
            along
            + full[..., 4 - distance : 4 - distance + extent_x, 4 : 4 + extent_y, 4 : 4 + extent_z]
        )
        along = (
            along
            + full[..., 4 : 4 + extent_x, 4 + distance : 4 + distance + extent_y, 4 : 4 + extent_z]
        )
        along = (
            along
            + full[..., 4 : 4 + extent_x, 4 - distance : 4 - distance + extent_y, 4 : 4 + extent_z]
        )
        along = (
            along
            + full[..., 4 : 4 + extent_x, 4 : 4 + extent_y, 4 + distance : 4 + distance + extent_z]
        )
        along = (
            along
            + full[..., 4 : 4 + extent_x, 4 : 4 + extent_y, 4 - distance : 4 - distance + extent_z]
        )
        totals = totals + stencil_taps[distance] * along
    return totals


def slab_mask(row_index, bounds):
    return ((row_index[None, :] >= bounds[:, 0:1]) & (row_index[None, :] < bounds[:, 1:2])).astype(
        jnp.float32
    )


def side_frame(field):
    return jnp.pad(field, ((0, 0), (0, 0), (4, 4), (4, 4)))


def local(probe_field, bounds, courant, snapshots, snap_times, basis_panels):
    probes_here, depth_rows, cells_y, cells_z = probe_field.shape
    steps_total = snap_times.shape[0]
    all_snaps = lax.all_gather(snapshots, "probe", axis=2, tiled=True)
    row_start = lax.axis_index("store") * depth_rows
    inside = slab_mask(row_start + jnp.arange(depth_rows, dtype=jnp.int32), bounds)
    perturb = probe_field.astype(jnp.float32) * inside[:, :, None, None]
    earlier = jnp.zeros((probes_here, depth_rows, cells_y, cells_z), jnp.float32)
    current = earlier
    for turn_index in range(steps_total):
        picked = lax.dynamic_index_in_dim(all_snaps, snap_times[turn_index], 0, keepdims=False)
        padded = extended(current, (("store", 1),), 4)
        advanced = (
            2.0 * current
            - earlier
            + courant * laplace(side_frame(padded))
            + perturb * picked.astype(jnp.float32)
        )
        earlier = current
        current = advanced
    response_low = current.astype(jnp.bfloat16)
    flat_fields = response_low.reshape(probes_here, -1)
    portion = lax.all_gather(basis_panels, "probe", axis=0, tiled=True)
    product = lax.dot_general(
        portion.reshape(portion.shape[0], -1),
        flat_fields,
        (((1,), (1,)), ((), ())),
        preferred_element_type=jnp.float32,
    )
    projection = lax.psum(product, "store")
    return (current, projection)


def solution(mesh):
    placed = (
        P("probe", "store", None, None),
        P("probe", None),
        P("store", None, None),
        P(None, "store", "probe", None),
        P(),
        P("probe", "store", None, None),
    )
    return jax.shard_map(
        local,
        mesh=mesh,
        in_specs=placed,
        out_specs=(P("probe", "store", None, None), P(None, "probe")),
        check_vma=False,
    )
```

profile of v0, /device:TPU:0, one launch (start us, length us, event | category | flops | bytes accessed | tf_op | source)
XLA Modules:
  0.0 564.6 jit_solution(12925683046278286328)
XLA Ops:
  26.5 6.3 %all_gather.6 = bf16[8,16,8,128]{3,1,0,2:T(8,128)(2,1)S(1)} all-gather(bf16[8,16,2,128]{3,1,0,2:T(8,128)(2,1)S(1)} %copy.10), channel_id=1, replica_groups=mesh['probe'=4,'store'=8] {'probe'}, dimensions={2}, use_global_device_ids=true | all-gather | bytes 327680 | tf_op jit(solution)/shard_map/all_gather | solution.py:69
  50.1 7.6 %collective-permute-done.2 = f32[24,4,8,128]{3,2,1,0:T(8,128)S(1)} collective-permute-done((f32[24,4,8,128]{3,2,1,0:T(8,128)S(1)}, f32[24,4,8,128]{3,2,1,0:T(8,128)S(1)}, u32[]{:S(2)}, u32[]{:S(2)}) %collective-permute-start.2) | collective-permute-done | bytes 393248 | tf_op jit(solution)/shard_map/ppermute | solution.py:17
  57.7 8.6 %collective-permute-done.3 = f32[24,4,8,128]{3,2,1,0:T(8,128)S(1)} collective-permute-done((f32[24,4,8,128]{3,2,1,0:T(8,128)S(1)}, f32[24,4,8,128]{3,2,1,0:T(8,128)S(1)}, u32[]{:S(2)}, u32[]{:S(2)}) %collective-permute-start.3) | collective-permute-done | bytes 393248 | tf_op jit(solution)/shard_map/ppermute | solution.py:16
  66.3 6.0 %select_maximum_fusion.12 = f32[24,24,16,136]{3,2,1,0:T(8,128)} fusion(f32[24,4,8,128]{3,2,1,0:T(8,128)S(1)} %collective-permute-done.2, f32[24,16,8,128]{3,2,1,0:T(8,128)S(1)} %fusion.231, f32[24,4,8,128]{3,2,1,0:T(8,128)S(1)} %collective-permute-done.3), kind=kLoop, calls=%fused_computation.32 | loop fusion | flops 18800640 | bytes 7372800 | tf_op jit(solution)/shard_map/concatenate | solution.py:18
  72.3 39.5 %fusion.200 = f32[24,16,8,128]{3,2,1,0:T(8,128)S(1)} fusion(f32[24,16,8,128]{3,2,1,0:T(8,128)} %copy-done.5, f32[24,4,8,128]{3,2,1,0:T(8,128)S(1)} %collective-permute-done.3, f32[24,4,8,128]{3,2,1,0:T(8,128)S(1)} %collective-permute-done.2, f32[24,24,16,136]{3,2,1,0:T(8,128)} %select_maximum_fusion.12, bf16[24,16,8,128]{3,2,1,0:T(8,128)(2,1)S(1)} %copy-done, ...), kind=kLoop, calls=%fused_computation.327 | loop fusion | flops 17301504 | bytes 30017024 | tf_op jit(solution)/shard_map/add | solution.py:79
  118.4 7.3 %collective-permute-done.4 = f32[24,4,8,128]{3,2,1,0:T(8,128)S(1)} collective-permute-done((f32[24,4,8,128]{3,2,1,0:T(8,128)S(1)}, f32[24,4,8,128]{3,2,1,0:T(8,128)S(1)}, u32[]{:S(2)}, u32[]{:S(2)}) %collective-permute-start.4) | collective-permute-done | bytes 393248 | tf_op jit(solution)/shard_map/ppermute | solution.py:17
  125.8 8.6 %collective-permute-done.5 = f32[24,4,8,128]{3,2,1,0:T(8,128)S(1)} collective-permute-done((f32[24,4,8,128]{3,2,1,0:T(8,128)S(1)}, f32[24,4,8,128]{3,2,1,0:T(8,128)S(1)}, u32[]{:S(2)}, u32[]{:S(2)}) %collective-permute-start.5) | collective-permute-done | bytes 393248 | tf_op jit(solution)/shard_map/ppermute | solution.py:16
  134.4 6.0 %select_maximum_fusion.10 = f32[24,24,16,136]{3,2,1,0:T(8,128)} fusion(f32[24,4,8,128]{3,2,1,0:T(8,128)S(1)} %collective-permute-done.4, f32[24,16,8,128]{3,2,1,0:T(8,128)S(1)} %fusion.200, f32[24,4,8,128]{3,2,1,0:T(8,128)S(1)} %collective-permute-done.5), kind=kLoop, calls=%fused_computation.30 | loop fusion | flops 18800640 | bytes 7372800 | tf_op jit(solution)/shard_map/concatenate | solution.py:18
  140.3 40.2 %fusion.169 = f32[24,16,8,128]{3,2,1,0:T(8,128)S(1)} fusion(f32[24,16,8,128]{3,2,1,0:T(8,128)} %copy-done.4, f32[24,4,8,128]{3,2,1,0:T(8,128)S(1)} %collective-permute-done.5, f32[24,4,8,128]{3,2,1,0:T(8,128)S(1)} %collective-permute-done.4, f32[24,24,16,136]{3,2,1,0:T(8,128)} %select_maximum_fusion.10, f32[24,16,8,128]{3,2,1,0:T(8,128)} %copy-done.5, ...), kind=kLoop, calls=%fused_computation.296 | loop fusion | flops 17694720 | bytes 31589888 | tf_op jit(solution)/shard_map/add | solution.py:79
  187.3 7.1 %collective-permute-done.6 = f32[24,4,8,128]{3,2,1,0:T(8,128)S(1)} collective-permute-done((f32[24,4,8,128]{3,2,1,0:T(8,128)S(1)}, f32[24,4,8,128]{3,2,1,0:T(8,128)S(1)}, u32[]{:S(2)}, u32[]{:S(2)}) %collective-permute-start.6) | collective-permute-done | bytes 393248 | tf_op jit(solution)/shard_map/ppermute | solution.py:17
  194.4 8.6 %collective-permute-done.7 = f32[24,4,8,128]{3,2,1,0:T(8,128)S(1)} collective-permute-done((f32[24,4,8,128]{3,2,1,0:T(8,128)S(1)}, f32[24,4,8,128]{3,2,1,0:T(8,128)S(1)}, u32[]{:S(2)}, u32[]{:S(2)}) %collective-permute-start.7) | collective-permute-done | bytes 393248 | tf_op jit(solution)/shard_map/ppermute | solution.py:16
  208.9 36.7 %fusion.138 = f32[24,16,8,128]{3,2,1,0:T(8,128)} fusion(f32[24,16,8,128]{3,2,1,0:T(8,128)S(1)} %fusion.169, f32[24,4,8,128]{3,2,1,0:T(8,128)S(1)} %collective-permute-done.7, f32[24,4,8,128]{3,2,1,0:T(8,128)S(1)} %collective-permute-done.6, f32[24,24,16,136]{3,2,1,0:T(8,128)} %select_maximum_fusion.8, f32[24,16,8,128]{3,2,1,0:T(8,128)} %copy-done.4, ...), kind=kLoop, calls=%fused_computation.265 | loop fusion | flops 17694720 | bytes 31589888 | tf_op jit(solution)/shard_map/add | solution.py:79
  253.3 7.3 %collective-permute-done.8 = f32[24,4,8,128]{3,2,1,0:T(8,128)S(1)} collective-permute-done((f32[24,4,8,128]{3,2,1,0:T(8,128)S(1)}, f32[24,4,8,128]{3,2,1,0:T(8,128)S(1)}, u32[]{:S(2)}, u32[]{:S(2)}) %collective-permute-start.8) | collective-permute-done | bytes 393248 | tf_op jit(solution)/shard_map/ppermute | solution.py:17
  260.6 8.6 %collective-permute-done.9 = f32[24,4,8,128]{3,2,1,0:T(8,128)S(1)} collective-permute-done((f32[24,4,8,128]{3,2,1,0:T(8,128)S(1)}, f32[24,4,8,128]{3,2,1,0:T(8,128)S(1)}, u32[]{:S(2)}, u32[]{:S(2)}) %collective-permute-start.9) | collective-permute-done | bytes 393248 | tf_op jit(solution)/shard_map/ppermute | solution.py:16
  275.2 39.8 %fusion.107 = f32[24,16,8,128]{3,2,1,0:T(8,128)S(1)} fusion(f32[24,16,8,128]{3,2,1,0:T(8,128)} %fusion.138, f32[24,4,8,128]{3,2,1,0:T(8,128)S(1)} %collective-permute-done.9, f32[24,4,8,128]{3,2,1,0:T(8,128)S(1)} %collective-permute-done.8, f32[24,24,16,136]{3,2,1,0:T(8,128)} %select_maximum_fusion.6, f32[24,16,8,128]{3,2,1,0:T(8,128)} %copy-done.2, ...), kind=kLoop, calls=%fused_computation.234 | loop fusion | flops 17694720 | bytes 31589888 | tf_op jit(solution)/shard_map/add | solution.py:79
  321.5 7.3 %collective-permute-done.10 = f32[24,4,8,128]{3,2,1,0:T(8,128)S(1)} collective-permute-done((f32[24,4,8,128]{3,2,1,0:T(8,128)S(1)}, f32[24,4,8,128]{3,2,1,0:T(8,128)S(1)}, u32[]{:S(2)}, u32[]{:S(2)}) %collective-permute-start.10) | collective-permute-done | bytes 393248 | tf_op jit(solution)/shard_map/ppermute | solution.py:17
  328.8 8.6 %collective-permute-done.11 = f32[24,4,8,128]{3,2,1,0:T(8,128)S(1)} collective-permute-done((f32[24,4,8,128]{3,2,1,0:T(8,128)S(1)}, f32[24,4,8,128]{3,2,1,0:T(8,128)S(1)}, u32[]{:S(2)}, u32[]{:S(2)}) %collective-permute-start.11) | collective-permute-done | bytes 393248 | tf_op jit(solution)/shard_map/ppermute | solution.py:16
  343.3 39.2 %fusion.76 = f32[24,16,8,128]{3,2,1,0:T(8,128)S(1)} fusion(f32[24,16,8,128]{3,2,1,0:T(8,128)} %copy-done.1, f32[24,4,8,128]{3,2,1,0:T(8,128)S(1)} %collective-permute-done.11, f32[24,4,8,128]{3,2,1,0:T(8,128)S(1)} %collective-permute-done.10, f32[24,24,16,136]{3,2,1,0:T(8,128)} %select_maximum_fusion.4, f32[24,16,8,128]{3,2,1,0:T(8,128)} %fusion.138, ...), kind=kLoop, calls=%fused_computation.203 | loop fusion | flops 17694720 | bytes 31589888 | tf_op jit(solution)/shard_map/add | solution.py:79
  397.4 8.7 %collective-permute-done.13 = f32[24,4,8,128]{3,2,1,0:T(8,128)S(1)} collective-permute-done((f32[24,4,8,128]{3,2,1,0:T(8,128)}, f32[24,4,8,128]{3,2,1,0:T(8,128)S(1)}, u32[]{:S(2)}, u32[]{:S(2)}) %collective-permute-start.13) | collective-permute-done | bytes 393248 | tf_op jit(solution)/shard_map/ppermute | solution.py:16
  412.0 36.5 %fusion.45 = f32[24,16,8,128]{3,2,1,0:T(8,128)} fusion(f32[24,16,8,128]{3,2,1,0:T(8,128)S(1)} %fusion.76, f32[24,4,8,128]{3,2,1,0:T(8,128)S(1)} %collective-permute-done.13, f32[24,4,8,128]{3,2,1,0:T(8,128)S(1)} %collective-permute-done.12, f32[24,24,16,136]{3,2,1,0:T(8,128)} %select_maximum_fusion.2, f32[24,16,8,128]{3,2,1,0:T(8,128)} %copy-done.1, ...), kind=kLoop, calls=%fused_computation.172 | loop fusion | flops 17694720 | bytes 31589888 | tf_op jit(solution)/shard_map/add | solution.py:79
  456.1 7.4 %collective-permute-done.14 = f32[24,4,8,128]{3,2,1,0:T(8,128)S(1)} collective-permute-done((f32[24,4,8,128]{3,2,1,0:T(8,128)S(1)}, f32[24,4,8,128]{3,2,1,0:T(8,128)S(1)}, u32[]{:S(2)}, u32[]{:S(2)}) %collective-permute-start.14) | collective-permute-done | bytes 393248 | tf_op jit(solution)/shard_map/ppermute | solution.py:17
  463.5 8.6 %collective-permute-done.15 = f32[24,4,8,128]{3,2,1,0:T(8,128)S(1)} collective-permute-done((f32[24,4,8,128]{3,2,1,0:T(8,128)S(1)}, f32[24,4,8,128]{3,2,1,0:T(8,128)S(1)}, u32[]{:S(2)}, u32[]{:S(2)}) %collective-permute-start.15) | collective-permute-done | bytes 393248 | tf_op jit(solution)/shard_map/ppermute | solution.py:16
  478.8 40.4 %fusion.265 = (bf16[24,16,8,128]{3,2,1,0:T(8,128)(2,1)S(1)}, f32[24,16,8,128]{3,2,1,0:T(8,128)}) fusion(f32[16,8,128]{2,1,0:T(8,128)S(1)} %copy.18, f32[24,16]{1,0:T(8,128)S(1)} %and_convert_fusion, bf16[24,16,8,128]{3,2,1,0:T(8,128)(2,1)S(1)} %copy-done, f32[24,24,16,136]{3,2,1,0:T(8,128)} %select_maximum_fusion, f32[24,16,8,128]{3,2,1,0:T(8,128)} %fusion.45, ...), kind=kLoop, calls=%fused_computation.448 | loop fusion | flops 18087936 | bytes 32376320 | tf_op jit(solution)/shard_map/convert_element_type | solution.py:86
  522.2 35.5 %psum.7 = f32[96,24]{0,1:T(8,128)} all-reduce(f32[96,24]{0,1:T(8,128)S(1)} %convolution_bitcast_fusion), channel_id=1, replica_groups=mesh['probe'=4,'store'=8] {'store'}, use_global_device_ids=true, to_apply=%region_0.1 | all-reduce | flops 2304 | bytes 18432 | tf_op jit(solution)/shard_map/psum | solution.py:95
  (83 shorter events, 104.8 us)
Async XLA Ops:
  7.2 31.4 %copy-start.13 = (s32[24,2]{0,1:T(2,128)S(1)}, s32[24,2]{0,1:T(2,128)}, u32[]{:S(2)}) copy-start(s32[24,2]{0,1:T(2,128)} %param.7) | copy-start | bytes 580
  7.2 512.0 %all-gather.2.cloned.1.call-start = ((), (), s32[]{:S(2)}) async-start(), calls=%async_computation | async-start | bytes 3932160 | tf_op jit(solution)/shard_map/all_gather | solution.py:88
  7.3 31.4 %collective-permute-start = (f32[24,4,8,128]{3,2,1,0:T(8,128)S(1)}, f32[24,4,8,128]{3,2,1,0:T(8,128)S(1)}, u32[]{:S(2)}, u32[]{:S(2)}) collective-permute-start(f32[24,4,8,128]{3,2,1,0:T(8,128)S(1)} %broadcast.90), channel_id=1, source_target_pairs={{1,0},{2,1},{3,2},{4,3},{5,4},{6,5},{7,6},{9,8},{10,9},{11,10},{12... | collective-permute-start | bytes 1179656 | tf_op jit(solution)/shard_map/ppermute | solution.py:17
  8.6 30.1 %collective-permute-start.1 = (f32[24,4,8,128]{3,2,1,0:T(8,128)S(1)}, f32[24,4,8,128]{3,2,1,0:T(8,128)S(1)}, u32[]{:S(2)}, u32[]{:S(2)}) collective-permute-start(f32[24,4,8,128]{3,2,1,0:T(8,128)S(1)} %broadcast.90), channel_id=1, source_target_pairs={{0,1},{1,2},{2,3},{3,4},{4,5},{5,6},{6,7},{8,9},{9,10},{10,11},{11... | collective-permute-start | bytes 1179656 | tf_op jit(solution)/shard_map/ppermute | solution.py:16
  43.8 22.6 %copy-start.5 = (f32[24,16,8,128]{3,2,1,0:T(8,128)}, f32[24,16,8,128]{3,2,1,0:T(8,128)S(1)}, u32[]{:S(2)}) copy-start(f32[24,16,8,128]{3,2,1,0:T(8,128)S(1)} %fusion.231) | copy-start | bytes 4718596
  43.8 13.9 %collective-permute-start.2 = (f32[24,4,8,128]{3,2,1,0:T(8,128)S(1)}, f32[24,4,8,128]{3,2,1,0:T(8,128)S(1)}, u32[]{:S(2)}, u32[]{:S(2)}) collective-permute-start(f32[24,4,8,128]{3,2,1,0:T(8,128)S(1)} %get-tuple-element.16), channel_id=1, source_target_pairs={{1,0},{2,1},{3,2},{4,3},{5,4},{6,5},{7,6},{9,8},{10,9},{11,10},{12... | collective-permute-start | bytes 1179656 | tf_op jit(solution)/shard_map/ppermute | solution.py:17
  45.1 21.2 %collective-permute-start.3 = (f32[24,4,8,128]{3,2,1,0:T(8,128)S(1)}, f32[24,4,8,128]{3,2,1,0:T(8,128)S(1)}, u32[]{:S(2)}, u32[]{:S(2)}) collective-permute-start(f32[24,4,8,128]{3,2,1,0:T(8,128)S(1)} %get-tuple-element.17), channel_id=1, source_target_pairs={{0,1},{1,2},{2,3},{3,4},{4,5},{5,6},{6,7},{8,9},{9,10},{10,11},{11... | collective-permute-start | bytes 1179656 | tf_op jit(solution)/shard_map/ppermute | solution.py:16
  111.9 22.5 %copy-start.4 = (f32[24,16,8,128]{3,2,1,0:T(8,128)}, f32[24,16,8,128]{3,2,1,0:T(8,128)S(1)}, u32[]{:S(2)}) copy-start(f32[24,16,8,128]{3,2,1,0:T(8,128)S(1)} %fusion.200) | copy-start | bytes 4718596
  112.0 13.8 %collective-permute-start.4 = (f32[24,4,8,128]{3,2,1,0:T(8,128)S(1)}, f32[24,4,8,128]{3,2,1,0:T(8,128)S(1)}, u32[]{:S(2)}, u32[]{:S(2)}) collective-permute-start(f32[24,4,8,128]{3,2,1,0:T(8,128)S(1)} %get-tuple-element.14), channel_id=1, source_target_pairs={{1,0},{2,1},{3,2},{4,3},{5,4},{6,5},{7,6},{9,8},{10,9},{11,10},{12... | collective-permute-start | bytes 1179656 | tf_op jit(solution)/shard_map/ppermute | solution.py:17
  113.4 21.0 %collective-permute-start.5 = (f32[24,4,8,128]{3,2,1,0:T(8,128)S(1)}, f32[24,4,8,128]{3,2,1,0:T(8,128)S(1)}, u32[]{:S(2)}, u32[]{:S(2)}) collective-permute-start(f32[24,4,8,128]{3,2,1,0:T(8,128)S(1)} %get-tuple-element.15), channel_id=1, source_target_pairs={{0,1},{1,2},{2,3},{3,4},{4,5},{5,6},{6,7},{8,9},{9,10},{10,11},{11... | collective-permute-start | bytes 1179656 | tf_op jit(solution)/shard_map/ppermute | solution.py:16
  180.5 28.5 %copy-start.2 = (f32[24,16,8,128]{3,2,1,0:T(8,128)}, f32[24,16,8,128]{3,2,1,0:T(8,128)S(1)}, u32[]{:S(2)}) copy-start(f32[24,16,8,128]{3,2,1,0:T(8,128)S(1)} %fusion.169) | copy-start | bytes 4718596
  180.6 13.8 %collective-permute-start.6 = (f32[24,4,8,128]{3,2,1,0:T(8,128)S(1)}, f32[24,4,8,128]{3,2,1,0:T(8,128)S(1)}, u32[]{:S(2)}, u32[]{:S(2)}) collective-permute-start(f32[24,4,8,128]{3,2,1,0:T(8,128)S(1)} %get-tuple-element.12), channel_id=1, source_target_pairs={{1,0},{2,1},{3,2},{4,3},{5,4},{6,5},{7,6},{9,8},{10,9},{11,10},{12... | collective-permute-start | bytes 1179656 | tf_op jit(solution)/shard_map/ppermute | solution.py:17
  182.0 21.0 %collective-permute-start.7 = (f32[24,4,8,128]{3,2,1,0:T(8,128)S(1)}, f32[24,4,8,128]{3,2,1,0:T(8,128)S(1)}, u32[]{:S(2)}, u32[]{:S(2)}) collective-permute-start(f32[24,4,8,128]{3,2,1,0:T(8,128)S(1)} %get-tuple-element.13), channel_id=1, source_target_pairs={{0,1},{1,2},{2,3},{3,4},{4,5},{5,6},{6,7},{8,9},{9,10},{10,11},{11... | collective-permute-start | bytes 1179656 | tf_op jit(solution)/shard_map/ppermute | solution.py:16
  245.6 23.6 %copy-start.3 = (f32[24,16,8,128]{3,2,1,0:T(8,128)S(1)}, f32[24,16,8,128]{3,2,1,0:T(8,128)}, u32[]{:S(2)}) copy-start(f32[24,16,8,128]{3,2,1,0:T(8,128)} %fusion.138) | copy-start | bytes 4718596
  246.9 13.7 %collective-permute-start.8 = (f32[24,4,8,128]{3,2,1,0:T(8,128)S(1)}, f32[24,4,8,128]{3,2,1,0:T(8,128)S(1)}, u32[]{:S(2)}, u32[]{:S(2)}) collective-permute-start(f32[24,4,8,128]{3,2,1,0:T(8,128)S(1)} %get-tuple-element.10), channel_id=1, source_target_pairs={{1,0},{2,1},{3,2},{4,3},{5,4},{6,5},{7,6},{9,8},{10,9},{11,10},{12... | collective-permute-start | bytes 1179656 | tf_op jit(solution)/shard_map/ppermute | solution.py:17
  248.2 21.0 %collective-permute-start.9 = (f32[24,4,8,128]{3,2,1,0:T(8,128)S(1)}, f32[24,4,8,128]{3,2,1,0:T(8,128)S(1)}, u32[]{:S(2)}, u32[]{:S(2)}) collective-permute-start(f32[24,4,8,128]{3,2,1,0:T(8,128)S(1)} %get-tuple-element.11), channel_id=1, source_target_pairs={{0,1},{1,2},{2,3},{3,4},{4,5},{5,6},{6,7},{8,9},{9,10},{10,11},{11... | collective-permute-start | bytes 1179656 | tf_op jit(solution)/shard_map/ppermute | solution.py:16
  315.0 22.3 %copy-start.1 = (f32[24,16,8,128]{3,2,1,0:T(8,128)}, f32[24,16,8,128]{3,2,1,0:T(8,128)S(1)}, u32[]{:S(2)}) copy-start(f32[24,16,8,128]{3,2,1,0:T(8,128)S(1)} %fusion.107) | copy-start | bytes 4718596
  315.1 13.7 %collective-permute-start.10 = (f32[24,4,8,128]{3,2,1,0:T(8,128)S(1)}, f32[24,4,8,128]{3,2,1,0:T(8,128)S(1)}, u32[]{:S(2)}, u32[]{:S(2)}) collective-permute-start(f32[24,4,8,128]{3,2,1,0:T(8,128)S(1)} %get-tuple-element.8), channel_id=1, source_target_pairs={{1,0},{2,1},{3,2},{4,3},{5,4},{6,5},{7,6},{9,8},{10,9},{11,10},{12... | collective-permute-start | bytes 1179656 | tf_op jit(solution)/shard_map/ppermute | solution.py:17
  316.4 21.0 %collective-permute-start.11 = (f32[24,4,8,128]{3,2,1,0:T(8,128)S(1)}, f32[24,4,8,128]{3,2,1,0:T(8,128)S(1)}, u32[]{:S(2)}, u32[]{:S(2)}) collective-permute-start(f32[24,4,8,128]{3,2,1,0:T(8,128)S(1)} %get-tuple-element.9), channel_id=1, source_target_pairs={{0,1},{1,2},{2,3},{3,4},{4,5},{5,6},{6,7},{8,9},{9,10},{10,11},{11... | collective-permute-start | bytes 1179656 | tf_op jit(solution)/shard_map/ppermute | solution.py:16
  383.5 13.9 %collective-permute-start.12 = (f32[24,4,8,128]{3,2,1,0:T(8,128)}, f32[24,4,8,128]{3,2,1,0:T(8,128)S(1)}, u32[]{:S(2)}, u32[]{:S(2)}) collective-permute-start(f32[24,4,8,128]{3,2,1,0:T(8,128)} %get-tuple-element.6), channel_id=1, source_target_pairs={{1,0},{2,1},{3,2},{4,3},{5,4},{6,5},{7,6},{9,8},{10,9},{11,10},{12... | collective-permute-start | bytes 1179656 | tf_op jit(solution)/shard_map/ppermute | solution.py:17
  384.8 21.3 %collective-permute-start.13 = (f32[24,4,8,128]{3,2,1,0:T(8,128)}, f32[24,4,8,128]{3,2,1,0:T(8,128)S(1)}, u32[]{:S(2)}, u32[]{:S(2)}) collective-permute-start(f32[24,4,8,128]{3,2,1,0:T(8,128)} %get-tuple-element.7), channel_id=1, source_target_pairs={{0,1},{1,2},{2,3},{3,4},{4,5},{5,6},{6,7},{8,9},{9,10},{10,11},{11... | collective-permute-start | bytes 1179656 | tf_op jit(solution)/shard_map/ppermute | solution.py:16
  448.5 24.3 %copy-start.6 = (f32[24,16,8,128]{3,2,1,0:T(8,128)S(1)}, f32[24,16,8,128]{3,2,1,0:T(8,128)}, u32[]{:S(2)}) copy-start(f32[24,16,8,128]{3,2,1,0:T(8,128)} %fusion.45) | copy-start | bytes 4718596
  449.8 13.7 %collective-permute-start.14 = (f32[24,4,8,128]{3,2,1,0:T(8,128)S(1)}, f32[24,4,8,128]{3,2,1,0:T(8,128)S(1)}, u32[]{:S(2)}, u32[]{:S(2)}) collective-permute-start(f32[24,4,8,128]{3,2,1,0:T(8,128)S(1)} %get-tuple-element.5), channel_id=1, source_target_pairs={{1,0},{2,1},{3,2},{4,3},{5,4},{6,5},{7,6},{9,8},{10,9},{11,10},{12... | collective-permute-start | bytes 1179656 | tf_op jit(solution)/shard_map/ppermute | solution.py:17
  451.1 21.0 %collective-permute-start.15 = (f32[24,4,8,128]{3,2,1,0:T(8,128)S(1)}, f32[24,4,8,128]{3,2,1,0:T(8,128)S(1)}, u32[]{:S(2)}, u32[]{:S(2)}) collective-permute-start(f32[24,4,8,128]{3,2,1,0:T(8,128)S(1)} %get-tuple-element.4), channel_id=1, source_target_pairs={{0,1},{1,2},{2,3},{3,4},{4,5},{5,6},{6,7},{8,9},{9,10},{10,11},{11... | collective-permute-start | bytes 1179656 | tf_op jit(solution)/shard_map/ppermute | solution.py:16
  (7 other events, 32.4 us)
Sparse Core Ops, SparseCore 0:
  391.6 30.1 all-gather.1
where the time goes:
time: 566 us; the launch traced here: 565 us
  other arithmetic  319 us (56%)
  waiting for transfers between devices  110 us (19%)
  starting transfers between devices  51.6 us (9%)
  blocking collectives  41.8 us (7%)
  between operations  29.4 us (5%)
  local copies, waits for them, and re-layouts  9.52 us (2%)
    add x7, other arithmetic, local(): 2.0 * current - earlier + courant * laplace(side_frame(padded))  236 us
    ppermute x8, waiting for transfers between devices, extended(): before = lax.ppermute(last, axis, up)  60.2 us
    ppermute x8, waiting for transfers between devices, extended(): after = lax.ppermute(leading, axis, down)  50 us
    concatenate x8, other arithmetic, extended(): x = jnp.concatenate([before, x, after], axis=dim)  42.1 us
    ppermute x8, starting transfers between devices, extended(): before = lax.ppermute(last, axis, up)  40.9 us
    convert_element_type x1, other arithmetic, local(): response_low = current.astype(jnp.bfloat16)  40.4 us
    psum x1, blocking collectives, local(): projection = lax.psum(product, 'store')  35.5 us
  transfers between devices with their start and end apart: 17, of which 14 were waited for; matrix products, arithmetic and copies ran while one was open for 17% of the time, Pallas kernels for 0%

commit v1 on v0

--- a/solution.py
+++ b/solution.py
@@ -4,6 +4,15 @@
 from jax.sharding import PartitionSpec as P
 
 stencil_taps = (-205.0 / 72.0, 8.0 / 5.0, -1.0 / 5.0, 8.0 / 315.0, -1.0 / 560.0)
+
+
+def doubling_sum(x, mesh_axis):
+    size = lax.axis_size(mesh_axis)
+    total, far = (x, 1)
+    while far < size:
+        total = total + lax.ppermute(total, mesh_axis, [(i, i ^ far) for i in range(size)])
+        far = 2 * far
+    return total
 
 
 def extended(x, sides, width):
@@ -92,7 +101,7 @@
         (((1,), (1,)), ((), ())),
         preferred_element_type=jnp.float32,
     )
-    projection = lax.psum(product, "store")
+    projection = doubling_sum(product, "store")
     return (current, projection)
 
 

time: 566 us -> 549 us (0.970)
  blocking collectives: 41.8 us -> 6.3 us
  other arithmetic: 319 us -> 326 us
  starting transfers between devices: 51.6 us -> 58.5 us
  waiting for transfers between devices: 110 us -> 116 us
    psum x1 -> x0, blocking collectives: 35.5 us -> none  [local(): projection = lax.psum(product, 'store')]
    ppermute x0 -> x3, starting transfers between devices: none -> 6.9 us  [doubling_sum(): lax.ppermute(total, mesh_axis, [(i, i ^ far) for i in range(size)])]
  transfers between devices with their start and end apart: 17 -> 20, of which waited for: 14 -> 17; matrix products, arithmetic and copies ran while one was open for 17% -> 18% of each run, Pallas kernels for 0% -> 0%
where the time goes in v1:
time: 549 us; the launch traced here: 548 us
  other arithmetic  326 us (59%)
  waiting for transfers between devices  116 us (21%)
  starting transfers between devices  58.5 us (11%)
  between operations  29.2 us (5%)
  local copies, waits for them, and re-layouts  9.53 us (2%)
  blocking collectives  6.3 us (1%)
    add x7, other arithmetic, local(): 2.0 * current - earlier + courant * laplace(side_frame(padded))  241 us
    ppermute x8, waiting for transfers between devices, extended(): before = lax.ppermute(last, axis, up)  60.2 us
    ppermute x8, waiting for transfers between devices, extended(): after = lax.ppermute(leading, axis, down)  49.9 us
    concatenate x8, other arithmetic, extended(): x = jnp.concatenate([before, x, after], axis=dim)  42.3 us
    convert_element_type x1, other arithmetic, local(): response_low = current.astype(jnp.bfloat16)  41.3 us
    ppermute x8, starting transfers between devices, extended(): before = lax.ppermute(last, axis, up)  40.9 us
  transfers between devices with their start and end apart: 20, of which 17 were waited for; matrix products, arithmetic and copies ran while one was open for 18% of the time, Pallas kernels for 0%

profile of v1, /device:TPU:0, one launch (start us, length us, event | category | flops | bytes accessed | tf_op | source)
XLA Modules:
  0.0 548.4 jit_solution(2628938198755227193)
XLA Ops:
  26.4 6.3 %all_gather.6 = bf16[8,16,8,128]{3,1,0,2:T(8,128)(2,1)S(1)} all-gather(bf16[8,16,2,128]{3,1,0,2:T(8,128)(2,1)S(1)} %copy.10), channel_id=1, replica_groups=mesh['probe'=4,'store'=8] {'probe'}, dimensions={2}, use_global_device_ids=true | all-gather | bytes 327680 | tf_op jit(solution)/shard_map/all_gather | solution.py:78
  50.0 7.6 %collective-permute-done.2 = f32[24,4,8,128]{3,2,1,0:T(8,128)S(1)} collective-permute-done((f32[24,4,8,128]{3,2,1,0:T(8,128)S(1)}, f32[24,4,8,128]{3,2,1,0:T(8,128)S(1)}, u32[]{:S(2)}, u32[]{:S(2)}) %collective-permute-start.2) | collective-permute-done | bytes 393248 | tf_op jit(solution)/shard_map/ppermute | solution.py:26
  57.6 8.6 %collective-permute-done.3 = f32[24,4,8,128]{3,2,1,0:T(8,128)S(1)} collective-permute-done((f32[24,4,8,128]{3,2,1,0:T(8,128)S(1)}, f32[24,4,8,128]{3,2,1,0:T(8,128)S(1)}, u32[]{:S(2)}, u32[]{:S(2)}) %collective-permute-start.3) | collective-permute-done | bytes 393248 | tf_op jit(solution)/shard_map/ppermute | solution.py:25
  66.2 6.0 %select_maximum_fusion.12 = f32[24,24,16,136]{3,2,1,0:T(8,128)} fusion(f32[24,4,8,128]{3,2,1,0:T(8,128)S(1)} %collective-permute-done.2, f32[24,16,8,128]{3,2,1,0:T(8,128)S(1)} %fusion.231, f32[24,4,8,128]{3,2,1,0:T(8,128)S(1)} %collective-permute-done.3), kind=kLoop, calls=%fused_computation.32 | loop fusion | flops 18800640 | bytes 7372800 | tf_op jit(solution)/shard_map/concatenate | solution.py:27
  72.2 40.5 %fusion.200 = f32[24,16,8,128]{3,2,1,0:T(8,128)S(1)} fusion(f32[24,16,8,128]{3,2,1,0:T(8,128)} %copy-done.5, f32[24,4,8,128]{3,2,1,0:T(8,128)S(1)} %collective-permute-done.3, f32[24,4,8,128]{3,2,1,0:T(8,128)S(1)} %collective-permute-done.2, f32[24,24,16,136]{3,2,1,0:T(8,128)} %select_maximum_fusion.12, bf16[24,16,8,128]{3,2,1,0:T(8,128)(2,1)S(1)} %copy-done, ...), kind=kLoop, calls=%fused_computation.327 | loop fusion | flops 17301504 | bytes 30017024 | tf_op jit(solution)/shard_map/add | solution.py:88
  119.3 7.3 %collective-permute-done.4 = f32[24,4,8,128]{3,2,1,0:T(8,128)S(1)} collective-permute-done((f32[24,4,8,128]{3,2,1,0:T(8,128)S(1)}, f32[24,4,8,128]{3,2,1,0:T(8,128)S(1)}, u32[]{:S(2)}, u32[]{:S(2)}) %collective-permute-start.4) | collective-permute-done | bytes 393248 | tf_op jit(solution)/shard_map/ppermute | solution.py:26
  126.6 8.6 %collective-permute-done.5 = f32[24,4,8,128]{3,2,1,0:T(8,128)S(1)} collective-permute-done((f32[24,4,8,128]{3,2,1,0:T(8,128)S(1)}, f32[24,4,8,128]{3,2,1,0:T(8,128)S(1)}, u32[]{:S(2)}, u32[]{:S(2)}) %collective-permute-start.5) | collective-permute-done | bytes 393248 | tf_op jit(solution)/shard_map/ppermute | solution.py:25
  135.2 6.0 %select_maximum_fusion.10 = f32[24,24,16,136]{3,2,1,0:T(8,128)} fusion(f32[24,4,8,128]{3,2,1,0:T(8,128)S(1)} %collective-permute-done.4, f32[24,16,8,128]{3,2,1,0:T(8,128)S(1)} %fusion.200, f32[24,4,8,128]{3,2,1,0:T(8,128)S(1)} %collective-permute-done.5), kind=kLoop, calls=%fused_computation.30 | loop fusion | flops 18800640 | bytes 7372800 | tf_op jit(solution)/shard_map/concatenate | solution.py:27
  141.2 41.1 %fusion.169 = f32[24,16,8,128]{3,2,1,0:T(8,128)S(1)} fusion(f32[24,16,8,128]{3,2,1,0:T(8,128)} %copy-done.4, f32[24,4,8,128]{3,2,1,0:T(8,128)S(1)} %collective-permute-done.5, f32[24,4,8,128]{3,2,1,0:T(8,128)S(1)} %collective-permute-done.4, f32[24,24,16,136]{3,2,1,0:T(8,128)} %select_maximum_fusion.10, f32[24,16,8,128]{3,2,1,0:T(8,128)} %copy-done.5, ...), kind=kLoop, calls=%fused_computation.296 | loop fusion | flops 17694720 | bytes 31589888 | tf_op jit(solution)/shard_map/add | solution.py:88
  189.1 7.1 %collective-permute-done.6 = f32[24,4,8,128]{3,2,1,0:T(8,128)S(1)} collective-permute-done((f32[24,4,8,128]{3,2,1,0:T(8,128)S(1)}, f32[24,4,8,128]{3,2,1,0:T(8,128)S(1)}, u32[]{:S(2)}, u32[]{:S(2)}) %collective-permute-start.6) | collective-permute-done | bytes 393248 | tf_op jit(solution)/shard_map/ppermute | solution.py:26
  196.2 8.6 %collective-permute-done.7 = f32[24,4,8,128]{3,2,1,0:T(8,128)S(1)} collective-permute-done((f32[24,4,8,128]{3,2,1,0:T(8,128)S(1)}, f32[24,4,8,128]{3,2,1,0:T(8,128)S(1)}, u32[]{:S(2)}, u32[]{:S(2)}) %collective-permute-start.7) | collective-permute-done | bytes 393248 | tf_op jit(solution)/shard_map/ppermute | solution.py:25
  210.7 37.7 %fusion.138 = f32[24,16,8,128]{3,2,1,0:T(8,128)} fusion(f32[24,16,8,128]{3,2,1,0:T(8,128)S(1)} %fusion.169, f32[24,4,8,128]{3,2,1,0:T(8,128)S(1)} %collective-permute-done.7, f32[24,4,8,128]{3,2,1,0:T(8,128)S(1)} %collective-permute-done.6, f32[24,24,16,136]{3,2,1,0:T(8,128)} %select_maximum_fusion.8, f32[24,16,8,128]{3,2,1,0:T(8,128)} %copy-done.4, ...), kind=kLoop, calls=%fused_computation.265 | loop fusion | flops 17694720 | bytes 31589888 | tf_op jit(solution)/shard_map/add | solution.py:88
  256.1 7.3 %collective-permute-done.8 = f32[24,4,8,128]{3,2,1,0:T(8,128)S(1)} collective-permute-done((f32[24,4,8,128]{3,2,1,0:T(8,128)S(1)}, f32[24,4,8,128]{3,2,1,0:T(8,128)S(1)}, u32[]{:S(2)}, u32[]{:S(2)}) %collective-permute-start.8) | collective-permute-done | bytes 393248 | tf_op jit(solution)/shard_map/ppermute | solution.py:26
  263.4 8.6 %collective-permute-done.9 = f32[24,4,8,128]{3,2,1,0:T(8,128)S(1)} collective-permute-done((f32[24,4,8,128]{3,2,1,0:T(8,128)S(1)}, f32[24,4,8,128]{3,2,1,0:T(8,128)S(1)}, u32[]{:S(2)}, u32[]{:S(2)}) %collective-permute-start.9) | collective-permute-done | bytes 393248 | tf_op jit(solution)/shard_map/ppermute | solution.py:25
  272.0 6.0 %select_maximum_fusion.6 = f32[24,24,16,136]{3,2,1,0:T(8,128)} fusion(f32[24,4,8,128]{3,2,1,0:T(8,128)S(1)} %collective-permute-done.8, f32[24,16,8,128]{3,2,1,0:T(8,128)S(1)} %copy-done.3, f32[24,4,8,128]{3,2,1,0:T(8,128)S(1)} %collective-permute-done.9), kind=kLoop, calls=%fused_computation.26 | loop fusion | flops 18800640 | bytes 7372800 | tf_op jit(solution)/shard_map/concatenate | solution.py:27
  278.0 40.8 %fusion.107 = f32[24,16,8,128]{3,2,1,0:T(8,128)S(1)} fusion(f32[24,16,8,128]{3,2,1,0:T(8,128)} %fusion.138, f32[24,4,8,128]{3,2,1,0:T(8,128)S(1)} %collective-permute-done.9, f32[24,4,8,128]{3,2,1,0:T(8,128)S(1)} %collective-permute-done.8, f32[24,24,16,136]{3,2,1,0:T(8,128)} %select_maximum_fusion.6, f32[24,16,8,128]{3,2,1,0:T(8,128)} %copy-done.2, ...), kind=kLoop, calls=%fused_computation.234 | loop fusion | flops 17694720 | bytes 31589888 | tf_op jit(solution)/shard_map/add | solution.py:88
  325.2 7.3 %collective-permute-done.10 = f32[24,4,8,128]{3,2,1,0:T(8,128)S(1)} collective-permute-done((f32[24,4,8,128]{3,2,1,0:T(8,128)S(1)}, f32[24,4,8,128]{3,2,1,0:T(8,128)S(1)}, u32[]{:S(2)}, u32[]{:S(2)}) %collective-permute-start.10) | collective-permute-done | bytes 393248 | tf_op jit(solution)/shard_map/ppermute | solution.py:26
  332.5 8.6 %collective-permute-done.11 = f32[24,4,8,128]{3,2,1,0:T(8,128)S(1)} collective-permute-done((f32[24,4,8,128]{3,2,1,0:T(8,128)S(1)}, f32[24,4,8,128]{3,2,1,0:T(8,128)S(1)}, u32[]{:S(2)}, u32[]{:S(2)}) %collective-permute-start.11) | collective-permute-done | bytes 393248 | tf_op jit(solution)/shard_map/ppermute | solution.py:25
  347.1 39.7 %fusion.76 = f32[24,16,8,128]{3,2,1,0:T(8,128)S(1)} fusion(f32[24,16,8,128]{3,2,1,0:T(8,128)} %copy-done.1, f32[24,4,8,128]{3,2,1,0:T(8,128)S(1)} %collective-permute-done.11, f32[24,4,8,128]{3,2,1,0:T(8,128)S(1)} %collective-permute-done.10, f32[24,24,16,136]{3,2,1,0:T(8,128)} %select_maximum_fusion.4, f32[24,16,8,128]{3,2,1,0:T(8,128)} %fusion.138, ...), kind=kLoop, calls=%fused_computation.203 | loop fusion | flops 17694720 | bytes 31589888 | tf_op jit(solution)/shard_map/add | solution.py:88
  401.7 8.7 %collective-permute-done.13 = f32[24,4,8,128]{3,2,1,0:T(8,128)S(1)} collective-permute-done((f32[24,4,8,128]{3,2,1,0:T(8,128)}, f32[24,4,8,128]{3,2,1,0:T(8,128)S(1)}, u32[]{:S(2)}, u32[]{:S(2)}) %collective-permute-start.13) | collective-permute-done | bytes 393248 | tf_op jit(solution)/shard_map/ppermute | solution.py:25
  416.3 37.5 %fusion.45 = f32[24,16,8,128]{3,2,1,0:T(8,128)} fusion(f32[24,16,8,128]{3,2,1,0:T(8,128)S(1)} %fusion.76, f32[24,4,8,128]{3,2,1,0:T(8,128)S(1)} %collective-permute-done.13, f32[24,4,8,128]{3,2,1,0:T(8,128)S(1)} %collective-permute-done.12, f32[24,24,16,136]{3,2,1,0:T(8,128)} %select_maximum_fusion.2, f32[24,16,8,128]{3,2,1,0:T(8,128)} %copy-done.1, ...), kind=kLoop, calls=%fused_computation.172 | loop fusion | flops 17694720 | bytes 31589888 | tf_op jit(solution)/shard_map/add | solution.py:88
  461.4 7.4 %collective-permute-done.14 = f32[24,4,8,128]{3,2,1,0:T(8,128)S(1)} collective-permute-done((f32[24,4,8,128]{3,2,1,0:T(8,128)S(1)}, f32[24,4,8,128]{3,2,1,0:T(8,128)S(1)}, u32[]{:S(2)}, u32[]{:S(2)}) %collective-permute-start.14) | collective-permute-done | bytes 393248 | tf_op jit(solution)/shard_map/ppermute | solution.py:26
  468.8 8.6 %collective-permute-done.15 = f32[24,4,8,128]{3,2,1,0:T(8,128)S(1)} collective-permute-done((f32[24,4,8,128]{3,2,1,0:T(8,128)S(1)}, f32[24,4,8,128]{3,2,1,0:T(8,128)S(1)}, u32[]{:S(2)}, u32[]{:S(2)}) %collective-permute-start.15) | collective-permute-done | bytes 393248 | tf_op jit(solution)/shard_map/ppermute | solution.py:25
  484.1 41.3 %fusion.265 = (bf16[24,16,8,128]{3,2,1,0:T(8,128)(2,1)S(1)}, f32[24,16,8,128]{3,2,1,0:T(8,128)}) fusion(f32[16,8,128]{2,1,0:T(8,128)S(1)} %copy.18, f32[24,16]{1,0:T(8,128)S(1)} %and_convert_fusion, bf16[24,16,8,128]{3,2,1,0:T(8,128)(2,1)S(1)} %copy-done, f32[24,24,16,136]{3,2,1,0:T(8,128)} %select_maximum_fusion, f32[24,16,8,128]{3,2,1,0:T(8,128)} %fusion.45, ...), kind=kLoop, calls=%fused_computation.448 | loop fusion | flops 18087936 | bytes 32376320 | tf_op jit(solution)/shard_map/convert_element_type | solution.py:95
  (91 shorter events, 112.0 us)
Async XLA Ops:
  7.2 31.3 %copy-start.13 = (s32[24,2]{0,1:T(2,128)S(1)}, s32[24,2]{0,1:T(2,128)}, u32[]{:S(2)}) copy-start(s32[24,2]{0,1:T(2,128)} %param.7) | copy-start | bytes 580
  7.2 518.3 %all-gather.2.cloned.1.call-start = ((), (), s32[]{:S(2)}) async-start(), calls=%async_computation | async-start | bytes 3932160 | tf_op jit(solution)/shard_map/all_gather | solution.py:97
  7.3 31.2 %collective-permute-start = (f32[24,4,8,128]{3,2,1,0:T(8,128)S(1)}, f32[24,4,8,128]{3,2,1,0:T(8,128)S(1)}, u32[]{:S(2)}, u32[]{:S(2)}) collective-permute-start(f32[24,4,8,128]{3,2,1,0:T(8,128)S(1)} %broadcast.90), channel_id=1, source_target_pairs={{1,0},{2,1},{3,2},{4,3},{5,4},{6,5},{7,6},{9,8},{10,9},{11,10},{12... | collective-permute-start | bytes 1179656 | tf_op jit(solution)/shard_map/ppermute | solution.py:26
  8.6 30.0 %collective-permute-start.1 = (f32[24,4,8,128]{3,2,1,0:T(8,128)S(1)}, f32[24,4,8,128]{3,2,1,0:T(8,128)S(1)}, u32[]{:S(2)}, u32[]{:S(2)}) collective-permute-start(f32[24,4,8,128]{3,2,1,0:T(8,128)S(1)} %broadcast.90), channel_id=1, source_target_pairs={{0,1},{1,2},{2,3},{3,4},{4,5},{5,6},{6,7},{8,9},{9,10},{10,11},{11... | collective-permute-start | bytes 1179656 | tf_op jit(solution)/shard_map/ppermute | solution.py:25
  43.7 13.9 %collective-permute-start.2 = (f32[24,4,8,128]{3,2,1,0:T(8,128)S(1)}, f32[24,4,8,128]{3,2,1,0:T(8,128)S(1)}, u32[]{:S(2)}, u32[]{:S(2)}) collective-permute-start(f32[24,4,8,128]{3,2,1,0:T(8,128)S(1)} %get-tuple-element.16), channel_id=1, source_target_pairs={{1,0},{2,1},{3,2},{4,3},{5,4},{6,5},{7,6},{9,8},{10,9},{11,10},{12... | collective-permute-start | bytes 1179656 | tf_op jit(solution)/shard_map/ppermute | solution.py:26
  45.0 21.2 %collective-permute-start.3 = (f32[24,4,8,128]{3,2,1,0:T(8,128)S(1)}, f32[24,4,8,128]{3,2,1,0:T(8,128)S(1)}, u32[]{:S(2)}, u32[]{:S(2)}) collective-permute-start(f32[24,4,8,128]{3,2,1,0:T(8,128)S(1)} %get-tuple-element.17), channel_id=1, source_target_pairs={{0,1},{1,2},{2,3},{3,4},{4,5},{5,6},{6,7},{8,9},{9,10},{10,11},{11... | collective-permute-start | bytes 1179656 | tf_op jit(solution)/shard_map/ppermute | solution.py:25
  112.8 13.8 %collective-permute-start.4 = (f32[24,4,8,128]{3,2,1,0:T(8,128)S(1)}, f32[24,4,8,128]{3,2,1,0:T(8,128)S(1)}, u32[]{:S(2)}, u32[]{:S(2)}) collective-permute-start(f32[24,4,8,128]{3,2,1,0:T(8,128)S(1)} %get-tuple-element.14), channel_id=1, source_target_pairs={{1,0},{2,1},{3,2},{4,3},{5,4},{6,5},{7,6},{9,8},{10,9},{11,10},{12... | collective-permute-start | bytes 1179656 | tf_op jit(solution)/shard_map/ppermute | solution.py:26
  114.2 21.0 %collective-permute-start.5 = (f32[24,4,8,128]{3,2,1,0:T(8,128)S(1)}, f32[24,4,8,128]{3,2,1,0:T(8,128)S(1)}, u32[]{:S(2)}, u32[]{:S(2)}) collective-permute-start(f32[24,4,8,128]{3,2,1,0:T(8,128)S(1)} %get-tuple-element.15), channel_id=1, source_target_pairs={{0,1},{1,2},{2,3},{3,4},{4,5},{5,6},{6,7},{8,9},{9,10},{10,11},{11... | collective-permute-start | bytes 1179656 | tf_op jit(solution)/shard_map/ppermute | solution.py:25
  182.3 28.5 %copy-start.2 = (f32[24,16,8,128]{3,2,1,0:T(8,128)}, f32[24,16,8,128]{3,2,1,0:T(8,128)S(1)}, u32[]{:S(2)}) copy-start(f32[24,16,8,128]{3,2,1,0:T(8,128)S(1)} %fusion.169) | copy-start | bytes 4718596
  182.4 13.8 %collective-permute-start.6 = (f32[24,4,8,128]{3,2,1,0:T(8,128)S(1)}, f32[24,4,8,128]{3,2,1,0:T(8,128)S(1)}, u32[]{:S(2)}, u32[]{:S(2)}) collective-permute-start(f32[24,4,8,128]{3,2,1,0:T(8,128)S(1)} %get-tuple-element.12), channel_id=1, source_target_pairs={{1,0},{2,1},{3,2},{4,3},{5,4},{6,5},{7,6},{9,8},{10,9},{11,10},{12... | collective-permute-start | bytes 1179656 | tf_op jit(solution)/shard_map/ppermute | solution.py:26
  183.8 21.0 %collective-permute-start.7 = (f32[24,4,8,128]{3,2,1,0:T(8,128)S(1)}, f32[24,4,8,128]{3,2,1,0:T(8,128)S(1)}, u32[]{:S(2)}, u32[]{:S(2)}) collective-permute-start(f32[24,4,8,128]{3,2,1,0:T(8,128)S(1)} %get-tuple-element.13), channel_id=1, source_target_pairs={{0,1},{1,2},{2,3},{3,4},{4,5},{5,6},{6,7},{8,9},{9,10},{10,11},{11... | collective-permute-start | bytes 1179656 | tf_op jit(solution)/shard_map/ppermute | solution.py:25
  248.4 23.6 %copy-start.3 = (f32[24,16,8,128]{3,2,1,0:T(8,128)S(1)}, f32[24,16,8,128]{3,2,1,0:T(8,128)}, u32[]{:S(2)}) copy-start(f32[24,16,8,128]{3,2,1,0:T(8,128)} %fusion.138) | copy-start | bytes 4718596
  249.7 13.7 %collective-permute-start.8 = (f32[24,4,8,128]{3,2,1,0:T(8,128)S(1)}, f32[24,4,8,128]{3,2,1,0:T(8,128)S(1)}, u32[]{:S(2)}, u32[]{:S(2)}) collective-permute-start(f32[24,4,8,128]{3,2,1,0:T(8,128)S(1)} %get-tuple-element.10), channel_id=1, source_target_pairs={{1,0},{2,1},{3,2},{4,3},{5,4},{6,5},{7,6},{9,8},{10,9},{11,10},{12... | collective-permute-start | bytes 1179656 | tf_op jit(solution)/shard_map/ppermute | solution.py:26
  251.0 21.0 %collective-permute-start.9 = (f32[24,4,8,128]{3,2,1,0:T(8,128)S(1)}, f32[24,4,8,128]{3,2,1,0:T(8,128)S(1)}, u32[]{:S(2)}, u32[]{:S(2)}) collective-permute-start(f32[24,4,8,128]{3,2,1,0:T(8,128)S(1)} %get-tuple-element.11), channel_id=1, source_target_pairs={{0,1},{1,2},{2,3},{3,4},{4,5},{5,6},{6,7},{8,9},{9,10},{10,11},{11... | collective-permute-start | bytes 1179656 | tf_op jit(solution)/shard_map/ppermute | solution.py:25
  318.8 13.7 %collective-permute-start.10 = (f32[24,4,8,128]{3,2,1,0:T(8,128)S(1)}, f32[24,4,8,128]{3,2,1,0:T(8,128)S(1)}, u32[]{:S(2)}, u32[]{:S(2)}) collective-permute-start(f32[24,4,8,128]{3,2,1,0:T(8,128)S(1)} %get-tuple-element.8), channel_id=1, source_target_pairs={{1,0},{2,1},{3,2},{4,3},{5,4},{6,5},{7,6},{9,8},{10,9},{11,10},{12... | collective-permute-start | bytes 1179656 | tf_op jit(solution)/shard_map/ppermute | solution.py:26
  320.1 21.0 %collective-permute-start.11 = (f32[24,4,8,128]{3,2,1,0:T(8,128)S(1)}, f32[24,4,8,128]{3,2,1,0:T(8,128)S(1)}, u32[]{:S(2)}, u32[]{:S(2)}) collective-permute-start(f32[24,4,8,128]{3,2,1,0:T(8,128)S(1)} %get-tuple-element.9), channel_id=1, source_target_pairs={{0,1},{1,2},{2,3},{3,4},{4,5},{5,6},{6,7},{8,9},{9,10},{10,11},{11... | collective-permute-start | bytes 1179656 | tf_op jit(solution)/shard_map/ppermute | solution.py:25
  387.8 13.9 %collective-permute-start.12 = (f32[24,4,8,128]{3,2,1,0:T(8,128)}, f32[24,4,8,128]{3,2,1,0:T(8,128)S(1)}, u32[]{:S(2)}, u32[]{:S(2)}) collective-permute-start(f32[24,4,8,128]{3,2,1,0:T(8,128)} %get-tuple-element.6), channel_id=1, source_target_pairs={{1,0},{2,1},{3,2},{4,3},{5,4},{6,5},{7,6},{9,8},{10,9},{11,10},{12... | collective-permute-start | bytes 1179656 | tf_op jit(solution)/shard_map/ppermute | solution.py:26
  389.1 21.3 %collective-permute-start.13 = (f32[24,4,8,128]{3,2,1,0:T(8,128)}, f32[24,4,8,128]{3,2,1,0:T(8,128)S(1)}, u32[]{:S(2)}, u32[]{:S(2)}) collective-permute-start(f32[24,4,8,128]{3,2,1,0:T(8,128)} %get-tuple-element.7), channel_id=1, source_target_pairs={{0,1},{1,2},{2,3},{3,4},{4,5},{5,6},{6,7},{8,9},{9,10},{10,11},{11... | collective-permute-start | bytes 1179656 | tf_op jit(solution)/shard_map/ppermute | solution.py:25
  453.8 24.3 %copy-start.6 = (f32[24,16,8,128]{3,2,1,0:T(8,128)S(1)}, f32[24,16,8,128]{3,2,1,0:T(8,128)}, u32[]{:S(2)}) copy-start(f32[24,16,8,128]{3,2,1,0:T(8,128)} %fusion.45) | copy-start | bytes 4718596
  455.1 13.7 %collective-permute-start.14 = (f32[24,4,8,128]{3,2,1,0:T(8,128)S(1)}, f32[24,4,8,128]{3,2,1,0:T(8,128)S(1)}, u32[]{:S(2)}, u32[]{:S(2)}) collective-permute-start(f32[24,4,8,128]{3,2,1,0:T(8,128)S(1)} %get-tuple-element.5), channel_id=1, source_target_pairs={{1,0},{2,1},{3,2},{4,3},{5,4},{6,5},{7,6},{9,8},{10,9},{11,10},{12... | collective-permute-start | bytes 1179656 | tf_op jit(solution)/shard_map/ppermute | solution.py:26
  456.4 21.0 %collective-permute-start.15 = (f32[24,4,8,128]{3,2,1,0:T(8,128)S(1)}, f32[24,4,8,128]{3,2,1,0:T(8,128)S(1)}, u32[]{:S(2)}, u32[]{:S(2)}) collective-permute-start(f32[24,4,8,128]{3,2,1,0:T(8,128)S(1)} %get-tuple-element.4), channel_id=1, source_target_pairs={{0,1},{1,2},{2,3},{3,4},{4,5},{5,6},{6,7},{8,9},{9,10},{10,11},{11... | collective-permute-start | bytes 1179656 | tf_op jit(solution)/shard_map/ppermute | solution.py:25
  528.5 4.2 collective-permute-start.16
  532.6 3.7 collective-permute-start.17
  536.3 4.6 collective-permute-start.18
  (10 other events, 99.8 us)
Sparse Core Ops, SparseCore 0:
  395.9 30.1 all-gather.1
